TPU v7x, 32 devices: a whole 2x2x4 slice. The times are simulated.
32 devices in a mesh: frame: 8 (over z, y), height: 4 (over x, core).
Axes of the slice: x: 2, y: 2, z: 4, core: 2. Of those that a mesh axis runs over, the one named last changes fastest.
Arguments:
- latents: bfloat16 [8, 24, 64, 1152], P('frame', 'height'), may hold values from -30 to 30
- qkv_weight: bfloat16 [2, 1152, 1728], replicated, as said below
- out_weight: bfloat16 [2, 576, 1152], replicated, may hold values from -0.25 to 0.25
Outputs:
- result: bfloat16 [8, 24, 64, 1152], P('frame', 'height')
Inputs may be any that keep to these rules, and one draw needn't show every extreme that they name: `qkv_weight`: entries lie within -0.2 to 0.2.
All inputs are finite; a program needn't handle non-finite values.
Results may differ from a plain program's by a relative error of at most 0.0095.
Values may be sent and summed in bfloat16 or wider, within the bound.
No kernel may reach another device: no remote copies, remote signals or barrier semaphores. Data moves between devices by JAX's collectives and lax.ppermute only.
A program may use at most 64 MiB of HBM per device.

v0:
```python
import jax
import jax.numpy as jnp
from jax import lax
from jax.sharding import PartitionSpec as P

HEAD_DIM = 72


def layer_norm(values):
    values = values.astype(jnp.float32)
    center = values - jnp.mean(values, axis=-1, keepdims=True)
    spread = jnp.mean(center * center, axis=-1, keepdims=True)
    return (center * lax.rsqrt(spread + 1e-06)).astype(jnp.bfloat16)


def project(tokens, weight):
    normed = layer_norm(tokens)
    flattened = normed.reshape(-1, normed.shape[-1])
    joined = jnp.dot(flattened, weight, preferred_element_type=jnp.float32)
    return joined.astype(jnp.bfloat16).reshape(tokens.shape[:-1] + (weight.shape[1],))


def attend(joined):
    length, batches = (joined.shape[0], joined.shape[1])
    inner_width = joined.shape[2] // 3
    head_count = inner_width // HEAD_DIM
    query_rows = joined[:, :, :inner_width].reshape(length, batches, head_count, HEAD_DIM)
    key_rows = joined[:, :, inner_width : 2 * inner_width].reshape(
        length, batches, head_count, HEAD_DIM
    )
    value_rows = joined[:, :, 2 * inner_width :].reshape(length, batches, head_count, HEAD_DIM)
    scores = jnp.einsum(
        "lbnd,mbnd->bnlm", query_rows, key_rows, preferred_element_type=jnp.float32
    ) * HEAD_DIM ** (-0.5)
    scores = scores - jnp.max(scores, axis=-1, keepdims=True)
    exponent = jnp.exp(scores)
    weights = (exponent / jnp.sum(exponent, axis=-1, keepdims=True)).astype(jnp.bfloat16)
    mixture = jnp.einsum("bnlm,mbnd->lbnd", weights, value_rows, preferred_element_type=jnp.float32)
    return mixture.reshape(length, batches, inner_width).astype(jnp.bfloat16)


def residual(tokens, mixture, weight):
    update = jnp.dot(
        mixture.reshape(-1, mixture.shape[-1]), weight, preferred_element_type=jnp.float32
    )
    return (tokens.astype(jnp.float32) + update.reshape(tokens.shape)).astype(jnp.bfloat16)


def frames_block(joined):
    length, single, places, triple = joined.shape
    mixture = attend(joined.reshape(length, single * places, triple))
    return mixture.reshape(length, single, places, triple // 3)


def per_device(latents, qkv_weight, out_weight):
    frames_dev, rows_dev, columns, feature_width = latents.shape
    frame_count = lax.axis_size("frame")
    rows_attend = jax.vmap(attend)
    rows_att = rows_attend(
        project(
            lax.all_to_all(latents, "height", split_axis=2, concat_axis=1, tiled=True),
            qkv_weight[0],
        )
    )
    rows_att = lax.all_to_all(rows_att, "height", split_axis=1, concat_axis=2, tiled=True)
    middle = residual(latents, rows_att, out_weight[0])
    places_dev = rows_dev * columns // frame_count
    grouped = middle.reshape(frames_dev, frame_count, places_dev, feature_width)
    frames_att = frames_block(
        project(
            lax.all_to_all(grouped, "frame", split_axis=1, concat_axis=0, tiled=True), qkv_weight[1]
        )
    )
    frames_att = lax.all_to_all(frames_att, "frame", split_axis=0, concat_axis=1, tiled=True)
    frames_att = frames_att.reshape(frames_dev, rows_dev, columns, frames_att.shape[-1])
    return residual(middle, frames_att, out_weight[1])


def solution(mesh):
    return jax.shard_map(
        per_device,
        mesh=mesh,
        in_specs=(P("frame", "height", None, None), P(), P()),
        out_specs=P("frame", "height", None, None),
        check_vma=False,
    )
```

profile of v0, /device:TPU:0, one launch (start us, length us, event | category | flops | bytes accessed | tf_op | source)
XLA Modules:
  0.0 113.4 jit_solution(6258203247795227640)
XLA Ops:
  0.0 1.7 %copy.33 = bf16[1,6,64,1152]{3,1,0,2:T(8,128)(2,1)S(1)} copy(bf16[1,6,64,1152]{3,2,1,0:T(8,128)(2,1)} %param.3) | data formatting | bytes 1769472 | tf_op args[0]
  1.7 20.1 %all_to_all.42 = bf16[1,6,64,1152]{3,1,0,2:T(8,128)(2,1)S(1)} all-to-all(bf16[1,6,64,1152]{3,1,0,2:T(8,128)(2,1)S(1)} %copy.33), channel_id=1, replica_groups=mesh['frame'=8,'height'=4] {'height'}, dimensions={2} | all-to-all | bytes 1769472 | tf_op jit(solution)/shard_map/all_to_all | solution.py:61
  21.9 0.2 fusion.24
  22.2 0.4 fusion.27
  22.5 0.3 fusion.28
  22.9 2.4 %fusion.12 = bf16[384,1728]{0,1:T(8,128)(2,1)S(1)} fusion(bf16[384,1152]{1,0:T(8,128)(2,1)S(1)} %bitcast.98, bf16[2,1152,1728]{1,2,0:T(8,128)(2,1)S(1)} %copy-done.5), kind=kOutput, calls=%fused_computation.14 | convolution fusion | flops 1529487360 | bytes 6193152 | tf_op jit(solution)/shard_map/dot_general | solution.py:19
  25.3 1.8 %copy.36 = bf16[384,1728]{1,0:T(8,128)(2,1)S(1)} copy(bf16[384,1728]{0,1:T(8,128)(2,1)S(1)} %fusion.12) | data formatting | bytes 2654208 | tf_op jit(solution)/shard_map/convert_element_type | solution.py:20
  27.1 0.3 fusion.68
  27.3 0.8 reshape.264
  28.1 0.8 reshape.265
  28.9 1.7 %reshape.263 = bf16[24,16,8,72]{3,2,1,0:T(8,128)(2,1)} reshape(bf16[1,24,16,576]{3,2,1,0:T(8,128)(2,1)S(1)} %get-tuple-element.8) | data formatting | bytes 884736 | tf_op jit(solution)/shard_map/reshape.7
  30.6 2.6 %fusion.69 = (f32[16,8,24]{2,1,0:T(8,128)S(1)}, f32[16,8,24,24]{2,3,1,0:T(8,128)}) fusion(bf16[24,16,8,72]{3,2,1,0:T(8,128)(2,1)S(1)} %reshape.265, bf16[24,16,8,72]{3,2,1,0:T(8,128)(2,1)S(1)} %reshape.264), kind=kOutput, calls=%fused_computation.65 | convolution fusion | flops 10838039 | bytes 1191936 | tf_op jit(solution)/shard_map/vmap()/sub | solution.py:35
  33.2 2.1 %fusion.37 = bf16[1,24,16,8,72]{4,1,3,2,0:T(8,128)(2,1)S(1)} fusion(f32[16,8,24,24]{2,3,1,0:T(8,128)} %get-tuple-element.12, bf16[24,16,8,72]{3,2,1,0:T(8,128)(2,1)S(1)} %copy-done.3, f32[16,8,24]{2,1,0:T(8,128)S(1)} %get-tuple-element.11), kind=kOutput, calls=%fused_computation.45 | convolution fusion | flops 10985472 | bytes 1191936 | tf_op jit(solution)/shard_map/vmap(bnlm,mbnd->lbnd)/dot_general | solution.py:38
  35.4 0.2 copy.41
  35.5 0.6 convert_element_type.136
  36.1 10.9 %all_to_all.43 = bf16[1,24,16,576]{3,2,0,1:T(8,128)(2,1)S(1)} all-to-all(bf16[1,24,16,576]{3,2,0,1:T(8,128)(2,1)S(1)} %bitcast.93), channel_id=1, replica_groups=mesh['frame'=8,'height'=4] {'height'}, dimensions={1} | all-to-all | bytes 884736 | tf_op jit(solution)/shard_map/all_to_all | solution.py:65
  47.0 2.3 %fusion.10 = bf16[1,6,64,1152]{3,2,1,0:T(8,128)(2,1)S(1)} fusion(bf16[6,64,576]{2,1,0:T(8,128)(2,1)S(1)} %bitcast.100, bf16[1,6,64,1152]{3,2,1,0:T(8,128)(2,1)S(1)} %copy-done.2, bf16[2,576,1152]{2,1,0:T(8,128)(2,1)} %param.5), kind=kOutput, calls=%fused_computation.12 | convolution fusion | flops 510935040 | bytes 3538944 | tf_op jit(solution)/shard_map/dot_general | solution.py:43
  49.3 28.1 %all_to_all.44 = bf16[1,8,48,1152]{3,2,0,1:T(8,128)(2,1)S(1)} all-to-all(bf16[1,8,48,1152]{3,2,0,1:T(8,128)(2,1)S(1)} %bitcast.96), channel_id=1, replica_groups=mesh['frame'=8,'height'=4] {'frame'}, dimensions={1} | all-to-all | bytes 1769472 | tf_op jit(solution)/shard_map/all_to_all | solution.py:71
  77.5 0.2 convert_reduce_fusion
  77.7 0.4 fusion.22
  78.1 0.3 fusion.19
  78.4 4.5 %fusion.15 = bf16[384,1728]{0,1:T(8,128)(2,1)S(1)} fusion(bf16[384,1152]{1,0:T(8,128)(2,1)S(1)} %bitcast.97, bf16[2,1152,1728]{1,2,0:T(8,128)(2,1)} %param.4), kind=kOutput, calls=%fused_computation.15 | convolution fusion | flops 1529487360 | bytes 6193152 | tf_op jit(solution)/shard_map/dot_general | solution.py:19
  82.8 1.8 %copy.45 = bf16[384,1728]{1,0:T(8,128)(2,1)S(1)} copy(bf16[384,1728]{0,1:T(8,128)(2,1)S(1)} %fusion.15) | data formatting | bytes 2654208 | tf_op jit(solution)/shard_map/convert_element_type | solution.py:20
  84.6 0.3 fusion.67
  84.9 0.8 reshape.269
  85.7 0.8 reshape.270
  86.5 1.7 %reshape.268 = bf16[8,48,8,72]{3,2,1,0:T(8,128)(2,1)} reshape(bf16[8,48,576]{2,1,0:T(8,128)(2,1)S(1)} %get-tuple-element.5) | data formatting | bytes 884736 | tf_op jit(solution)/shard_map/reshape | solution.py:31
  88.1 2.8 %fusion.74 = (f32[48,8,8]{2,1,0:T(8,128)S(1)}, f32[48,8,8,8]{2,3,1,0:T(8,128)}) fusion(bf16[8,48,8,72]{3,2,1,0:T(8,128)(2,1)S(1)} %reshape.270, bf16[8,48,8,72]{3,2,1,0:T(8,128)(2,1)S(1)} %reshape.269), kind=kOutput, calls=%fused_computation.66 | convolution fusion | flops 3612679 | bytes 995328 | tf_op jit(solution)/shard_map/sub | solution.py:35
  90.9 2.2 %fusion.38 = bf16[8,48,8,72]{3,0,2,1:T(8,128)(2,1)S(1)} fusion(f32[48,8,8,8]{2,3,1,0:T(8,128)} %get-tuple-element.14, bf16[8,48,8,72]{3,2,1,0:T(8,128)(2,1)S(1)} %copy-done.4, f32[48,8,8]{2,1,0:T(8,128)S(1)} %get-tuple-element.13), kind=kOutput, calls=%fused_computation.46 | convolution fusion | flops 3809280 | bytes 995328 | tf_op jit(solution)/shard_map/bnlm,mbnd->lbnd/dot_general | solution.py:38
  93.2 0.6 convert_element_type.147
  93.8 16.4 %all_to_all.45 = bf16[8,1,48,576]{3,2,1,0:T(8,128)(2,1)S(1)} all-to-all(bf16[8,1,48,576]{3,2,1,0:T(8,128)(2,1)S(1)} %bitcast.95), channel_id=1, replica_groups=mesh['frame'=8,'height'=4] {'frame'}, dimensions={0} | all-to-all | bytes 884736 | tf_op jit(solution)/shard_map/all_to_all | solution.py:74
  110.2 3.2 %fusion.11 = bf16[1,6,64,1152]{3,2,1,0:T(8,128)(2,1)} fusion(bf16[6,64,576]{2,1,0:T(8,128)(2,1)S(1)} %bitcast.99, bf16[1,6,64,1152]{3,2,1,0:T(8,128)(2,1)S(1)} %copy-done.1, bf16[2,576,1152]{2,1,0:T(8,128)(2,1)} %param.5), kind=kOutput, calls=%fused_computation.13 | convolution fusion | flops 510935040 | bytes 3538944 | tf_op jit(solution)/shard_map/dot_general | solution.py:43
  (20 shorter events, 0.4 us)
Async XLA Ops:
  1.7 21.2 %copy-start.5 = (bf16[2,1152,1728]{1,2,0:T(8,128)(2,1)S(1)}, bf16[2,1152,1728]{1,2,0:T(8,128)(2,1)}, u32[]{:S(2)}) copy-start(bf16[2,1152,1728]{1,2,0:T(8,128)(2,1)} %param.4) | copy-start | bytes 23887876
  30.6 2.6 %copy-start.3 = (bf16[24,16,8,72]{3,2,1,0:T(8,128)(2,1)S(1)}, bf16[24,16,8,72]{3,2,1,0:T(8,128)(2,1)}, u32[]{:S(2)}) copy-start(bf16[24,16,8,72]{3,2,1,0:T(8,128)(2,1)} %reshape.263) | copy-start | bytes 1327108
  35.5 11.5 %copy-start.2 = (bf16[1,6,64,1152]{3,2,1,0:T(8,128)(2,1)S(1)}, bf16[1,6,64,1152]{3,2,1,0:T(8,128)(2,1)}, u32[]{:S(2)}) copy-start(bf16[1,6,64,1152]{3,2,1,0:T(8,128)(2,1)} %param.3) | copy-start | bytes 2654212
  49.3 28.7 %copy-start = (bf16[1,6,64,1152]{3,2,1,0:T(8,128)(2,1)}, bf16[1,6,64,1152]{3,2,1,0:T(8,128)(2,1)S(1)}, u32[]{:S(2)}) copy-start(bf16[1,6,64,1152]{3,2,1,0:T(8,128)(2,1)S(1)} %fusion.10) | copy-start | bytes 2654212
  88.1 2.8 %copy-start.4 = (bf16[8,48,8,72]{3,2,1,0:T(8,128)(2,1)S(1)}, bf16[8,48,8,72]{3,2,1,0:T(8,128)(2,1)}, u32[]{:S(2)}) copy-start(bf16[8,48,8,72]{3,2,1,0:T(8,128)(2,1)} %reshape.268) | copy-start | bytes 1327108
  93.1 17.1 %copy-start.1 = (bf16[1,6,64,1152]{3,2,1,0:T(8,128)(2,1)S(1)}, bf16[1,6,64,1152]{3,2,1,0:T(8,128)(2,1)}, u32[]{:S(2)}) copy-start(bf16[1,6,64,1152]{3,2,1,0:T(8,128)(2,1)} %copy-done) | copy-start | bytes 2654212
where the time goes:
time: 114 us; the launch traced here: 113 us
  blocking collectives  75.5 us (66%)
  matrix products  22 us (19%)
  local copies, waits for them, and re-layouts  13.9 us (12%)
  other arithmetic  1.71 us (2%)
    all_to_all x1, blocking collectives, per_device(): lax.all_to_all(grouped, 'frame', split_axis=1, concat_axis=0, tiled=True)  28.1 us
    all_to_all x1, blocking collectives, per_device(): lax.all_to_all(latents, 'height', split_axis=2, concat_axis=1, tiled=True)  20.1 us
    all_to_all x1, blocking collectives, per_device(): lax.all_to_all(frames_att, 'frame', split_axis=0, concat_axis=1, tiled=True)  16.4 us
    all_to_all x1, blocking collectives, per_device(): lax.all_to_all(rows_att, 'height', split_axis=1, concat_axis=2, tiled=True)  10.9 us
    dot_general x2, matrix products, project(): joined = jnp.dot(flattened, weight, preferred_element_type=jnp.float32)  6.84 us
    dot_general x2, matrix products, residual(): jnp.dot(mixture.reshape(-1, mixture.shape[-1]), weight, preferred_element...  5.45 us
    sub x2, matrix products, attend(): scores = scores - jnp.max(scores, axis=-1, keepdims=True)  5.41 us
    dot_general x2, matrix products, attend(): jnp.einsum('bnlm,mbnd->lbnd', weights, value_rows, preferred_element_type...  4.31 us

commit v1 on v0

--- a/solution.py
+++ b/solution.py
@@ -4,6 +4,39 @@
 from jax.sharding import PartitionSpec as P
 
 HEAD_DIM = 72
+
+
+def sides_watch(x_local, axis_k, sheet):
+    block_last = x_local.shape
+    main = x_local.reshape(
+        *block_last[:axis_k], sheet, block_last[axis_k] // sheet, *block_last[axis_k + 1 :]
+    )
+    even = jnp.moveaxis(main, axis_k, 0)
+    return even
+
+
+def carry_table_in(target, dim_k):
+    extra = list(target.shape[1:])
+    extra[dim_k] *= target.shape[0]
+    local_now = jnp.moveaxis(target, 0, dim_k).reshape(extra)
+    return local_now
+
+
+def sizes_make(my_data, group_axis, shard_in, array_here):
+    s_next, piece_now = (lax.axis_size(group_axis), lax.axis_index(group_axis))
+    inter = sides_watch(my_data, shard_in, s_next)
+    a_now = inter
+    k0 = 1
+    while k0 < s_next:
+        block_out, reached = ((piece_now + k0) % s_next, (piece_now - k0) % s_next)
+        v_now = lax.dynamic_index_in_dim(inter, block_out, 0)
+        latest = lax.ppermute(
+            v_now, axis_name=group_axis, perm=tuple(((q, (q + k0) % s_next) for q in range(s_next)))
+        )
+        a_now = lax.dynamic_update_slice_in_dim(a_now, latest, reached, axis=0)
+        k0 += 1
+    out_arr = carry_table_in(a_now, array_here)
+    return out_arr
 
 
 def layer_norm(values):
@@ -71,7 +104,7 @@
             lax.all_to_all(grouped, "frame", split_axis=1, concat_axis=0, tiled=True), qkv_weight[1]
         )
     )
-    frames_att = lax.all_to_all(frames_att, "frame", split_axis=0, concat_axis=1, tiled=True)
+    frames_att = sizes_make(frames_att, "frame", 0, 1)
     frames_att = frames_att.reshape(frames_dev, rows_dev, columns, frames_att.shape[-1])
     return residual(middle, frames_att, out_weight[1])
 

time: 114 us -> 112 us (0.982)
  blocking collectives: 75.5 us -> 31 us
  waiting for transfers between devices: 0 us -> 25.5 us
  starting transfers between devices: 0 us -> 15.7 us
    all_to_all x2 -> x0, blocking collectives: 44.5 us -> none  [the longest x1 28.1 us: per_device(): lax.all_to_all(grouped, 'frame', split_axis=1, concat_axis=0, tiled=True)]
    all_to_all x0 -> x1, waiting for transfers between devices: none -> 22.2 us  [per_device(): lax.all_to_all(grouped, 'frame', split_axis=1, concat_axis=0, tiled=True)]
    ppermute x0 -> x7, starting transfers between devices: none -> 9.83 us  [sizes_make(): lax.ppermute(v_now, axis_name=group_axis, perm=tuple(((q, (q + k0) % s_ne...]
    all_to_all x0 -> x1, starting transfers between devices: none -> 5.82 us  [per_device(): lax.all_to_all(grouped, 'frame', split_axis=1, concat_axis=0, tiled=True)]
    ppermute x0 -> x7, waiting for transfers between devices: none -> 3.31 us  [sizes_make(): lax.ppermute(v_now, axis_name=group_axis, perm=tuple(((q, (q + k0) % s_ne...]
  transfers between devices with their start and end apart: 0 -> 8, of which waited for: 0 -> 4; matrix products, arithmetic and copies ran while one was open for 0% -> 1% of each run, Pallas kernels for 0% -> 0%
where the time goes in v1:
time: 112 us
  blocking collectives  31 us (28%)
  waiting for transfers between devices  25.5 us (23%)
  matrix products  23.1 us (21%)
  starting transfers between devices  15.7 us (14%)
  local copies, waits for them, and re-layouts  14.6 us (13%)
  other arithmetic  1.72 us (2%)
    all_to_all x1, waiting for transfers between devices, per_device(): lax.all_to_all(grouped, 'frame', split_axis=1, concat_axis=0, tiled=True)  22.2 us
    all_to_all x1, blocking collectives, per_device(): lax.all_to_all(latents, 'height', split_axis=2, concat_axis=1, tiled=True)  20.1 us
    all_to_all x1, blocking collectives, per_device(): lax.all_to_all(rows_att, 'height', split_axis=1, concat_axis=2, tiled=True)  10.9 us
    ppermute x7, starting transfers between devices, sizes_make(): lax.ppermute(v_now, axis_name=group_axis, perm=tuple(((q, (q + k0) % s_ne...  9.83 us
    dot_general x2, matrix products, project(): joined = jnp.dot(flattened, weight, preferred_element_type=jnp.float32)  6.85 us
    dot_general x2, matrix products, residual(): jnp.dot(mixture.reshape(-1, mixture.shape[-1]), weight, preferred_element...  6.59 us
    all_to_all x1, starting transfers between devices, per_device(): lax.all_to_all(grouped, 'frame', split_axis=1, concat_axis=0, tiled=True)  5.82 us
    sub x2, matrix products, attend(): scores = scores - jnp.max(scores, axis=-1, keepdims=True)  5.41 us
  transfers between devices with their start and end apart: 8, of which 4 were waited for; matrix products, arithmetic and copies ran while one was open for 1% of the time, Pallas kernels for 0%

profile of v1, /device:TPU:0, one launch (start us, length us, event | category | flops | bytes accessed | tf_op | source)
XLA Modules:
  0.0 111.9 jit_solution(4870966234256798093)
XLA Ops:
  0.0 1.7 %copy.35 = bf16[1,6,64,1152]{3,1,0,2:T(8,128)(2,1)S(1)} copy(bf16[1,6,64,1152]{3,2,1,0:T(8,128)(2,1)} %param.3) | data formatting | bytes 1769472 | tf_op args[0]
  1.7 20.1 %all_to_all.33 = bf16[1,6,64,1152]{3,1,0,2:T(8,128)(2,1)S(1)} all-to-all(bf16[1,6,64,1152]{3,1,0,2:T(8,128)(2,1)S(1)} %copy.35), channel_id=1, replica_groups=mesh['frame'=8,'height'=4] {'height'}, dimensions={2} | all-to-all | bytes 1769472 | tf_op jit(solution)/shard_map/all_to_all | solution.py:94
  22.9 2.4 %fusion.12 = bf16[384,1728]{0,1:T(8,128)(2,1)S(1)} fusion(bf16[384,1152]{1,0:T(8,128)(2,1)S(1)} %bitcast.111, bf16[2,1152,1728]{1,2,0:T(8,128)(2,1)S(1)} %copy-done.3), kind=kOutput, calls=%fused_computation.14 | convolution fusion | flops 1529487360 | bytes 6193152 | tf_op jit(solution)/shard_map/dot_general | solution.py:52
  25.3 1.8 %copy.38 = bf16[384,1728]{1,0:T(8,128)(2,1)S(1)} copy(bf16[384,1728]{0,1:T(8,128)(2,1)S(1)} %fusion.12) | data formatting | bytes 2654208 | tf_op jit(solution)/shard_map/convert_element_type | solution.py:53
  27.3 0.8 reshape.267
  28.1 0.8 reshape.268
  28.9 1.7 %reshape.266 = bf16[24,16,8,72]{3,2,1,0:T(8,128)(2,1)} reshape(bf16[1,24,16,576]{3,2,1,0:T(8,128)(2,1)S(1)} %get-tuple-element.8) | data formatting | bytes 884736 | tf_op jit(solution)/shard_map/reshape.7
  30.6 2.6 %fusion.69 = (f32[16,8,24]{2,1,0:T(8,128)S(1)}, f32[16,8,24,24]{2,3,1,0:T(8,128)}) fusion(bf16[24,16,8,72]{3,2,1,0:T(8,128)(2,1)S(1)} %reshape.268, bf16[24,16,8,72]{3,2,1,0:T(8,128)(2,1)S(1)} %reshape.267), kind=kOutput, calls=%fused_computation.79 | convolution fusion | flops 10838039 | bytes 1191936 | tf_op jit(solution)/shard_map/vmap()/sub | solution.py:68
  33.2 2.1 %fusion.37 = bf16[1,24,16,8,72]{4,1,3,2,0:T(8,128)(2,1)S(1)} fusion(f32[16,8,24,24]{2,3,1,0:T(8,128)} %get-tuple-element.19, bf16[24,16,8,72]{3,2,1,0:T(8,128)(2,1)S(1)} %copy-done.1, f32[16,8,24]{2,1,0:T(8,128)S(1)} %get-tuple-element.18), kind=kOutput, calls=%fused_computation.45 | convolution fusion | flops 10985472 | bytes 1191936 | tf_op jit(solution)/shard_map/vmap(bnlm,mbnd->lbnd)/dot_general | solution.py:71
  36.1 10.9 %all_to_all.34 = bf16[1,24,16,576]{3,2,0,1:T(8,128)(2,1)S(1)} all-to-all(bf16[1,24,16,576]{3,2,0,1:T(8,128)(2,1)S(1)} %bitcast.108), channel_id=1, replica_groups=mesh['frame'=8,'height'=4] {'height'}, dimensions={1} | all-to-all | bytes 884736 | tf_op jit(solution)/shard_map/all_to_all | solution.py:98
  47.0 3.2 %fusion.10 = bf16[1,6,64,1152]{3,2,1,0:T(8,128)(2,1)} fusion(bf16[6,64,576]{2,1,0:T(8,128)(2,1)S(1)} %bitcast.113, bf16[1,6,64,1152]{3,2,1,0:T(8,128)(2,1)S(1)} %copy-done, bf16[2,576,1152]{2,1,0:T(8,128)(2,1)} %param.5), kind=kOutput, calls=%fused_computation.12 | convolution fusion | flops 510935040 | bytes 3538944 | tf_op jit(solution)/shard_map/dot_general | solution.py:76
  50.2 5.8 %all-to-all-start.2 = ((bf16[1,8,48,1152]{3,2,0,1:T(8,128)(2,1)}), bf16[1,8,48,1152]{3,2,0,1:T(8,128)(2,1)S(1)}, u32[]{:S(2)}, u32[]{:S(2)}) async-start(bf16[1,8,48,1152]{3,2,0,1:T(8,128)(2,1)} %bitcast.16), calls=%async_computation.2 | async-start | bytes 1769472 | tf_op jit(solution)/shard_map/all_to_all | solution.py:104
  56.1 22.2 %all-to-all-done.2 = bf16[1,8,48,1152]{3,2,0,1:T(8,128)(2,1)S(1)} async-done(((bf16[1,8,48,1152]{3,2,0,1:T(8,128)(2,1)}), bf16[1,8,48,1152]{3,2,0,1:T(8,128)(2,1)S(1)}, u32[]{:S(2)}, u32[]{:S(2)}) %all-to-all-start.2) | async-done | bytes 884768 | tf_op jit(solution)/shard_map/all_to_all | solution.py:104
  79.2 4.5 %fusion.15 = bf16[384,1728]{0,1:T(8,128)(2,1)S(1)} fusion(bf16[384,1152]{1,0:T(8,128)(2,1)S(1)} %bitcast.110, bf16[2,1152,1728]{1,2,0:T(8,128)(2,1)} %param.4), kind=kOutput, calls=%fused_computation.15 | convolution fusion | flops 1529487360 | bytes 6193152 | tf_op jit(solution)/shard_map/dot_general | solution.py:52
  83.6 1.8 %copy.47 = bf16[384,1728]{1,0:T(8,128)(2,1)S(1)} copy(bf16[384,1728]{0,1:T(8,128)(2,1)S(1)} %fusion.15) | data formatting | bytes 2654208 | tf_op jit(solution)/shard_map/convert_element_type | solution.py:53
  85.7 0.8 reshape.272
  86.5 0.8 reshape.273
  87.3 1.7 %reshape.271 = bf16[8,48,8,72]{3,2,1,0:T(8,128)(2,1)} reshape(bf16[8,48,576]{2,1,0:T(8,128)(2,1)S(1)} %get-tuple-element.5) | data formatting | bytes 884736 | tf_op jit(solution)/shard_map/reshape | solution.py:64
  88.9 2.8 %fusion.74 = (f32[48,8,8]{2,1,0:T(8,128)S(1)}, f32[48,8,8,8]{2,3,1,0:T(8,128)}) fusion(bf16[8,48,8,72]{3,2,1,0:T(8,128)(2,1)S(1)} %reshape.273, bf16[8,48,8,72]{3,2,1,0:T(8,128)(2,1)S(1)} %reshape.272), kind=kOutput, calls=%fused_computation.80 | convolution fusion | flops 3612679 | bytes 995328 | tf_op jit(solution)/shard_map/sub | solution.py:68
  91.7 2.2 %fusion.38 = bf16[8,48,8,72]{3,0,2,1:T(8,128)(2,1)S(1)} fusion(f32[48,8,8,8]{2,3,1,0:T(8,128)} %get-tuple-element.21, bf16[8,48,8,72]{3,2,1,0:T(8,128)(2,1)S(1)} %copy-done.2, f32[48,8,8]{2,1,0:T(8,128)S(1)} %get-tuple-element.20), kind=kOutput, calls=%fused_computation.46 | convolution fusion | flops 3809280 | bytes 995328 | tf_op jit(solution)/shard_map/bnlm,mbnd->lbnd/dot_general | solution.py:71
  94.0 0.6 convert_element_type.152
  94.7 1.3 %collective-permute-start = (bf16[1,1,1,48,576]{4,3,0,2,1:T(8,128)(2,1)S(1)}, bf16[1,1,1,48,576]{4,3,0,2,1:T(8,128)(2,1)S(1)}, u32[]{:S(2)}, u32[]{:S(2)}) collective-permute-start(bf16[1,1,1,48,576]{4,3,0,2,1:T(8,128)(2,1)S(1)} %get-tuple-element.17), channel_id=1, source_target_pairs={{0,4},{4,8},{8,12},{12,16},{16,20},{20,24},{24,28},{28,0},{1,5},{5... | collective-permute-start | bytes 165896 | tf_op jit(solution)/shard_map/ppermute | solution.py:33
  95.9 0.6 convert_element_type.151
  96.6 1.7 %collective-permute-start.2 = (bf16[1,1,1,48,576]{4,3,0,2,1:T(8,128)(2,1)S(1)}, bf16[1,1,1,48,576]{4,3,0,2,1:T(8,128)(2,1)S(1)}, u32[]{:S(2)}, u32[]{:S(2)}) collective-permute-start(bf16[1,1,1,48,576]{4,3,0,2,1:T(8,128)(2,1)S(1)} %get-tuple-element.15), channel_id=1, source_target_pairs={{0,12},{4,16},{8,20},{12,24},{16,28},{20,0},{24,4},{28,8},{1,13},{... | collective-permute-start | bytes 165896 | tf_op jit(solution)/shard_map/ppermute | solution.py:33
  98.3 2.4 %collective-permute-start.3 = (bf16[1,1,1,48,576]{4,3,0,2,1:T(8,128)(2,1)S(1)}, bf16[1,1,1,48,576]{4,3,0,2,1:T(8,128)(2,1)S(1)}, u32[]{:S(2)}, u32[]{:S(2)}) collective-permute-start(bf16[1,1,1,48,576]{4,3,0,2,1:T(8,128)(2,1)S(1)} %get-tuple-element.14), channel_id=1, source_target_pairs={{0,16},{4,20},{8,24},{12,28},{16,0},{20,4},{24,8},{28,12},{1,17},{... | collective-permute-start | bytes 165896 | tf_op jit(solution)/shard_map/ppermute | solution.py:33
  100.7 1.7 %collective-permute-start.4 = (bf16[1,1,1,48,576]{4,3,0,2,1:T(8,128)(2,1)S(1)}, bf16[1,1,1,48,576]{4,3,0,2,1:T(8,128)(2,1)S(1)}, u32[]{:S(2)}, u32[]{:S(2)}) collective-permute-start(bf16[1,1,1,48,576]{4,3,0,2,1:T(8,128)(2,1)S(1)} %get-tuple-element.13), channel_id=1, source_target_pairs={{0,20},{4,24},{8,28},{12,0},{16,4},{20,8},{24,12},{28,16},{1,21},{... | collective-permute-start | bytes 165896 | tf_op jit(solution)/shard_map/ppermute | solution.py:33
  102.4 1.8 %collective-permute-start.5 = (bf16[1,1,1,48,576]{4,3,0,2,1:T(8,128)(2,1)S(1)}, bf16[1,1,1,48,576]{4,3,0,2,1:T(8,128)(2,1)S(1)}, u32[]{:S(2)}, u32[]{:S(2)}) collective-permute-start(bf16[1,1,1,48,576]{4,3,0,2,1:T(8,128)(2,1)S(1)} %get-tuple-element.12), channel_id=1, source_target_pairs={{0,24},{4,28},{8,0},{12,4},{16,8},{20,12},{24,16},{28,20},{1,25},{... | collective-permute-start | bytes 165896 | tf_op jit(solution)/shard_map/ppermute | solution.py:33
  104.2 0.9 collective-permute-start.6
  105.2 1.2 %collective-permute-done.3 = bf16[1,1,1,48,576]{4,3,0,2,1:T(8,128)(2,1)S(1)} collective-permute-done((bf16[1,1,1,48,576]{4,3,0,2,1:T(8,128)(2,1)S(1)}, bf16[1,1,1,48,576]{4,3,0,2,1:T(8,128)(2,1)S(1)}, u32[]{:S(2)}, u32[]{:S(2)}) %collective-permute-start.3) | collective-permute-done | bytes 55328 | tf_op jit(solution)/shard_map/ppermute | solution.py:33
  106.4 1.2 %collective-permute-done.4 = bf16[1,1,1,48,576]{4,3,0,2,1:T(8,128)(2,1)S(1)} collective-permute-done((bf16[1,1,1,48,576]{4,3,0,2,1:T(8,128)(2,1)S(1)}, bf16[1,1,1,48,576]{4,3,0,2,1:T(8,128)(2,1)S(1)}, u32[]{:S(2)}, u32[]{:S(2)}) %collective-permute-start.4) | collective-permute-done | bytes 55328 | tf_op jit(solution)/shard_map/ppermute | solution.py:33
  107.6 0.9 collective-permute-done.6
  108.5 3.4 %fusion.11 = bf16[1,6,64,1152]{3,2,1,0:T(8,128)(2,1)} fusion(bf16[6,64,576]{2,1,0:T(8,128)(2,1)S(1)} %bitcast.112, bf16[1,6,64,1152]{3,2,1,0:T(8,128)(2,1)} %fusion.10, bf16[2,576,1152]{2,1,0:T(8,128)(2,1)} %param.5), kind=kOutput, calls=%fused_computation.13 | convolution fusion | flops 510935040 | bytes 3538944 | tf_op jit(solution)/shard_map/dot_general | solution.py:76
  (39 shorter events, 3.6 us)
Async XLA Ops:
  1.7 21.2 %copy-start.3 = (bf16[2,1152,1728]{1,2,0:T(8,128)(2,1)S(1)}, bf16[2,1152,1728]{1,2,0:T(8,128)(2,1)}, u32[]{:S(2)}) copy-start(bf16[2,1152,1728]{1,2,0:T(8,128)(2,1)} %param.4) | copy-start | bytes 23887876
  30.6 2.6 %copy-start.1 = (bf16[24,16,8,72]{3,2,1,0:T(8,128)(2,1)S(1)}, bf16[24,16,8,72]{3,2,1,0:T(8,128)(2,1)}, u32[]{:S(2)}) copy-start(bf16[24,16,8,72]{3,2,1,0:T(8,128)(2,1)} %reshape.266) | copy-start | bytes 1327108
  35.5 11.5 %copy-start = (bf16[1,6,64,1152]{3,2,1,0:T(8,128)(2,1)S(1)}, bf16[1,6,64,1152]{3,2,1,0:T(8,128)(2,1)}, u32[]{:S(2)}) copy-start(bf16[1,6,64,1152]{3,2,1,0:T(8,128)(2,1)} %param.3) | copy-start | bytes 2654212
  50.2 28.0 %all-to-all-start.2 = ((bf16[1,8,48,1152]{3,2,0,1:T(8,128)(2,1)}), bf16[1,8,48,1152]{3,2,0,1:T(8,128)(2,1)S(1)}, u32[]{:S(2)}, u32[]{:S(2)}) async-start(bf16[1,8,48,1152]{3,2,0,1:T(8,128)(2,1)} %bitcast.16), calls=%async_computation.2 | async-start | bytes 1769472 | tf_op jit(solution)/shard_map/all_to_all | solution.py:104
  88.9 2.8 %copy-start.2 = (bf16[8,48,8,72]{3,2,1,0:T(8,128)(2,1)S(1)}, bf16[8,48,8,72]{3,2,1,0:T(8,128)(2,1)}, u32[]{:S(2)}) copy-start(bf16[8,48,8,72]{3,2,1,0:T(8,128)(2,1)} %reshape.271) | copy-start | bytes 1327108
  94.7 7.8 %collective-permute-start = (bf16[1,1,1,48,576]{4,3,0,2,1:T(8,128)(2,1)S(1)}, bf16[1,1,1,48,576]{4,3,0,2,1:T(8,128)(2,1)S(1)}, u32[]{:S(2)}, u32[]{:S(2)}) collective-permute-start(bf16[1,1,1,48,576]{4,3,0,2,1:T(8,128)(2,1)S(1)} %get-tuple-element.17), channel_id=1, source_target_pairs={{0,4},{4,8},{8,12},{12,16},{16,20},{20,24},{24,28},{28,0},{1,5},{5... | collective-permute-start | bytes 165896 | tf_op jit(solution)/shard_map/ppermute | solution.py:33
  96.5 7.7 %collective-permute-start.1 = (bf16[1,1,1,48,576]{4,3,0,2,1:T(8,128)(2,1)S(1)}, bf16[1,1,1,48,576]{4,3,0,2,1:T(8,128)(2,1)S(1)}, u32[]{:S(2)}, u32[]{:S(2)}) collective-permute-start(bf16[1,1,1,48,576]{4,3,0,2,1:T(8,128)(2,1)S(1)} %get-tuple-element.16), channel_id=1, source_target_pairs={{0,8},{4,12},{8,16},{12,20},{16,24},{20,28},{24,0},{28,4},{1,9},{5... | collective-permute-start | bytes 165896 | tf_op jit(solution)/shard_map/ppermute | solution.py:33
  96.6 8.5 %collective-permute-start.2 = (bf16[1,1,1,48,576]{4,3,0,2,1:T(8,128)(2,1)S(1)}, bf16[1,1,1,48,576]{4,3,0,2,1:T(8,128)(2,1)S(1)}, u32[]{:S(2)}, u32[]{:S(2)}) collective-permute-start(bf16[1,1,1,48,576]{4,3,0,2,1:T(8,128)(2,1)S(1)} %get-tuple-element.15), channel_id=1, source_target_pairs={{0,12},{4,16},{8,20},{12,24},{16,28},{20,0},{24,4},{28,8},{1,13},{... | collective-permute-start | bytes 165896 | tf_op jit(solution)/shard_map/ppermute | solution.py:33
  98.3 8.0 %collective-permute-start.3 = (bf16[1,1,1,48,576]{4,3,0,2,1:T(8,128)(2,1)S(1)}, bf16[1,1,1,48,576]{4,3,0,2,1:T(8,128)(2,1)S(1)}, u32[]{:S(2)}, u32[]{:S(2)}) collective-permute-start(bf16[1,1,1,48,576]{4,3,0,2,1:T(8,128)(2,1)S(1)} %get-tuple-element.14), channel_id=1, source_target_pairs={{0,16},{4,20},{8,24},{12,28},{16,0},{20,4},{24,8},{28,12},{1,17},{... | collective-permute-start | bytes 165896 | tf_op jit(solution)/shard_map/ppermute | solution.py:33
  100.7 6.9 %collective-permute-start.4 = (bf16[1,1,1,48,576]{4,3,0,2,1:T(8,128)(2,1)S(1)}, bf16[1,1,1,48,576]{4,3,0,2,1:T(8,128)(2,1)S(1)}, u32[]{:S(2)}, u32[]{:S(2)}) collective-permute-start(bf16[1,1,1,48,576]{4,3,0,2,1:T(8,128)(2,1)S(1)} %get-tuple-element.13), channel_id=1, source_target_pairs={{0,20},{4,24},{8,28},{12,0},{16,4},{20,8},{24,12},{28,16},{1,21},{... | collective-permute-start | bytes 165896 | tf_op jit(solution)/shard_map/ppermute | solution.py:33
  102.4 5.2 %collective-permute-start.5 = (bf16[1,1,1,48,576]{4,3,0,2,1:T(8,128)(2,1)S(1)}, bf16[1,1,1,48,576]{4,3,0,2,1:T(8,128)(2,1)S(1)}, u32[]{:S(2)}, u32[]{:S(2)}) collective-permute-start(bf16[1,1,1,48,576]{4,3,0,2,1:T(8,128)(2,1)S(1)} %get-tuple-element.12), channel_id=1, source_target_pairs={{0,24},{4,28},{8,0},{12,4},{16,8},{20,12},{24,16},{28,20},{1,25},{... | collective-permute-start | bytes 165896 | tf_op jit(solution)/shard_map/ppermute | solution.py:33
  104.2 4.3 %collective-permute-start.6 = (bf16[1,1,1,48,576]{4,3,0,2,1:T(8,128)(2,1)S(1)}, bf16[1,1,1,48,576]{4,3,0,2,1:T(8,128)(2,1)S(1)}, u32[]{:S(2)}, u32[]{:S(2)}) collective-permute-start(bf16[1,1,1,48,576]{4,3,0,2,1:T(8,128)(2,1)S(1)} %get-tuple-element.11), channel_id=1, source_target_pairs={{0,28},{4,0},{8,4},{12,8},{16,12},{20,16},{24,20},{28,24},{1,29},{... | collective-permute-start | bytes 165896 | tf_op jit(solution)/shard_map/ppermute | solution.py:33
